TPU v7x, 32 devices: a whole 2x2x4 slice. The times are simulated.
32 devices in a mesh: parts: 2 (over y), seq: 16 (over z, x, core).
Axes of the slice: x: 2, y: 2, z: 4, core: 2. Of those that a mesh axis runs over, the one named last changes fastest.
Arguments:
- queries: bfloat16 [32, 8192], P(('parts', 'seq')), parts along dimension 0, may hold values from -140 to 140
- new_keys: bfloat16 [32, 1024], P(('parts', 'seq')), parts along dimension 0, may hold values from -7 to 7
- new_values: bfloat16 [32, 1024], P(('parts', 'seq')), parts along dimension 0, may hold values from -6 to 6
- doc_keys: bfloat16 [32768, 1024], P(('parts', 'seq')), parts along dimension 0, may hold values from -6 to 6
- doc_values: bfloat16 [32768, 1024], P(('parts', 'seq')), parts along dimension 0, may hold values from -6 to 6
- suffix_keys: bfloat16 [32768, 1024], P(('parts', 'seq')), parts along dimension 0, may hold values from -6 to 6
- suffix_values: bfloat16 [32768, 1024], P(('parts', 'seq')), parts along dimension 0, may hold values from -6 to 6
- keep_lists: int32 [32, 32], P(('parts', 'seq')), parts along dimension 0, may hold values from 0 to 127, as said below
- suffix_lengths: int32 [16], P('parts'), parts along dimension 0, may hold values from 1 to 2048
Outputs:
- attended: bfloat16 [32, 8192], P(('parts', 'seq')), parts along dimension 0
There are 2 independent parts, one for each index of `parts`. A program takes and returns all parts, laid end to end along the dimension named above; each array names one. Nothing has to cross between parts.
Inputs may be any that keep to these rules, and one draw needn't show every extreme that they name: Row r's list (rows 2r and 2r+1 of keep_lists) names 64 different blocks of 0 to 127.
All inputs are finite; a program needn't handle non-finite values.
Results may differ from a plain program's by a relative error of at most 0.007.
Values may be sent and summed in bfloat16 or wider, within the bound.
No kernel may reach another device: no remote copies, remote signals or barrier semaphores. Data moves between devices by JAX's collectives and lax.ppermute only.
A program may use at most 128 MiB of HBM per device.

v0:
```python
import jax
import jax.numpy as jnp
from jax import lax
from jax.sharding import PartitionSpec as P

HEADS = 64
KVH = 8
HD = 128
BLOCK = 128
NEG_BIG = -1e30


def merge_terms(first, second):
    ceiling = jnp.maximum(first[0], second[0])
    left_scale = jnp.exp(first[0] - ceiling)
    right_scale = jnp.exp(second[0] - ceiling)
    return (
        ceiling,
        left_scale * first[1] + right_scale * second[1],
        left_scale[..., None] * first[2] + right_scale[..., None] * second[2],
    )


def block_terms(scores, live_keys, value_rows, form):
    masked = jnp.where(live_keys, scores, NEG_BIG)
    block_max = jnp.max(masked, axis=-1)
    weights = jnp.where(live_keys, jnp.exp(scores - block_max[..., None]), 0.0)
    block_sum = jnp.sum(weights, axis=-1)
    block_out = jnp.einsum(
        form, weights.astype(jnp.bfloat16), value_rows, preferred_element_type=jnp.float32
    )
    global_maximum = jnp.max(block_max, axis=-1)
    factor = jnp.exp(block_max - global_maximum[..., None])
    return (
        global_maximum,
        jnp.sum(factor * block_sum, axis=-1),
        jnp.sum(factor[..., None] * block_out, axis=-2),
    )


def per_device(
    queries,
    new_keys,
    new_values,
    doc_keys,
    doc_values,
    suffix_keys,
    suffix_values,
    keep_lists,
    suffix_lengths,
):
    groups = HEADS // KVH
    factor_scale = HD ** (-0.5)
    devices = lax.axis_size("seq")
    my_index = lax.axis_index("seq")
    row_id = my_index // 2
    parity = my_index % 2
    blocks_here = doc_keys.shape[0] // BLOCK
    gathered = lax.all_gather(queries, "seq", axis=0, tiled=True)
    every_list = lax.all_gather(keep_lists, "seq", axis=0, tiled=True)
    local_ids = every_list.reshape(devices // 2, -1) - my_index * blocks_here
    block_range = jnp.arange(blocks_here, dtype=jnp.int32)
    row_hits = jnp.any(local_ids[:, :, None] == block_range[None, None, :], axis=1)
    token_mask = jnp.repeat(row_hits, 2, axis=0)
    q_heads = gathered.reshape(devices, KVH, groups, HD).transpose(1, 0, 2, 3)
    key_heads = doc_keys.reshape(blocks_here, BLOCK, KVH, HD).transpose(2, 0, 1, 3)
    value_heads = doc_values.reshape(blocks_here, BLOCK, KVH, HD).transpose(2, 0, 1, 3)

    def doc_head(head_item):
        q_part, key_part, value_part = head_item
        scores = (
            jnp.einsum("tgd,bjd->tgbj", q_part, key_part, preferred_element_type=jnp.float32)
            * factor_scale
        )
        return block_terms(scores, token_mask[:, None, :, None], value_part, "tgbj,bjd->tgbd")

    doc_max, doc_sum, doc_out = lax.map(doc_head, (q_heads, key_heads, value_heads))
    doc_partial = (
        doc_max.transpose(1, 0, 2).reshape(devices, HEADS),
        doc_sum.transpose(1, 0, 2).reshape(devices, HEADS),
        doc_out.transpose(1, 0, 2, 3).reshape(devices, HEADS, HD),
    )
    q_rows = lax.dynamic_slice_in_dim(gathered, 2 * row_id, 2, 0).reshape(2, KVH, groups, HD)
    suffix_here = suffix_keys.shape[0]
    suffix_blocks = suffix_here // BLOCK
    keys_suf = suffix_keys.reshape(suffix_blocks, BLOCK, KVH, HD)
    values_suf = suffix_values.reshape(suffix_blocks, BLOCK, KVH, HD)
    scores = (
        jnp.einsum("tkgd,bjkd->tkgbj", q_rows, keys_suf, preferred_element_type=jnp.float32)
        * factor_scale
    )
    position = parity * suffix_here + jnp.arange(suffix_here, dtype=jnp.int32).reshape(
        suffix_blocks, BLOCK
    )
    live_keys = position < suffix_lengths[row_id]
    row_partial = block_terms(scores, live_keys, values_suf, "tkgbj,bjkd->tkgbd")
    own_scores = (
        jnp.einsum(
            "tkgd,kd->tkg", q_rows, new_keys.reshape(KVH, HD), preferred_element_type=jnp.float32
        )
        * factor_scale
    )
    visible = jnp.broadcast_to(
        (jnp.arange(2, dtype=jnp.int32) >= parity)[:, None, None], own_scores.shape
    )
    own_values = jnp.broadcast_to(
        new_values.reshape(KVH, HD).astype(jnp.float32)[None, :, None, :], (2, KVH, groups, HD)
    )
    own_partial = (
        jnp.where(visible, own_scores, NEG_BIG),
        visible.astype(jnp.float32),
        jnp.where(visible[..., None], own_values, 0.0),
    )
    row_partial = merge_terms(row_partial, own_partial)
    placed = (
        lax.dynamic_update_slice(
            jnp.full((devices, HEADS), NEG_BIG, jnp.float32),
            row_partial[0].reshape(2, HEADS),
            (2 * row_id, 0),
        ),
        lax.dynamic_update_slice(
            jnp.zeros((devices, HEADS), jnp.float32),
            row_partial[1].reshape(2, HEADS),
            (2 * row_id, 0),
        ),
        lax.dynamic_update_slice(
            jnp.zeros((devices, HEADS, HD), jnp.float32),
            row_partial[2].reshape(2, HEADS, HD),
            (2 * row_id, 0, 0),
        ),
    )
    span_max, span_sum, span_out = merge_terms(doc_partial, placed)
    units = (span_out / jnp.maximum(span_sum, 1.0)[..., None]).astype(jnp.bfloat16)
    parts_max, parts_sum = (
        lax.all_to_all(span_max[:, None, :], "seq", split_axis=0, concat_axis=1, tiled=True),
        lax.all_to_all(span_sum[:, None, :], "seq", split_axis=0, concat_axis=1, tiled=True),
    )
    parts_unit = lax.all_to_all(
        units.reshape(devices, 1, HEADS * HD), "seq", split_axis=0, concat_axis=1, tiled=True
    )
    ceiling = jnp.max(parts_max, axis=1)
    weight = jnp.exp(parts_max - ceiling[:, None, :]) * parts_sum
    total_sum = jnp.sum(weight, axis=1)
    total_out = jnp.sum(
        weight[..., None] * parts_unit.reshape(1, devices, HEADS, HD).astype(jnp.float32), axis=1
    )
    return (total_out / total_sum[..., None]).reshape(1, HEADS * HD).astype(jnp.bfloat16)


def solution(mesh):
    in_specs = (
        P(("parts", "seq"), None),
        P(("parts", "seq"), None),
        P(("parts", "seq"), None),
        P(("parts", "seq"), None),
        P(("parts", "seq"), None),
        P(("parts", "seq"), None),
        P(("parts", "seq"), None),
        P(("parts", "seq"), None),
        P("parts"),
    )
    out_specs = P(("parts", "seq"), None)
    return jax.shard_map(
        per_device, mesh=mesh, in_specs=in_specs, out_specs=out_specs, check_vma=False
    )
```

profile of v0, /device:TPU:0, one launch (start us, length us, event | category | flops | bytes accessed | tf_op | source)
XLA Modules:
  0.0 115.1 jit_solution(774386942064762164)
XLA Ops:
  0.0 24.8 %all-gather.1 = bf16[16,1,8192]{2,1,0:T(2,128)(2,1)S(1)} all-gather(bf16[1,1,8192]{2,1,0:T(2,128)(2,1)} %bitcast.210), channel_id=1, replica_groups=mesh['parts'=2,'seq'=16] {'seq'}, dimensions={0}, use_global_device_ids=true | all-gather | bytes 278528 | tf_op jit(solution)/shard_map/all_gather | solution.py:59
  24.8 2.2 %copy.160 = bf16[128,8,8,128]{3,2,1,0:T(8,128)(2,1)S(1)} copy(bf16[128,8,8,128]{3,1,2,0:T(8,128)(2,1)} %bitcast.191) | data formatting | bytes 4194304
  28.4 0.7 add_compare_fusion
  29.3 0.8 select_reduce_fusion.2
  30.1 0.9 fusion.38
  31.1 0.7 fusion.54
  32.1 17.4 %all-gather = s32[16,1,32]{2,1,0:T(1,128)S(1)} all-gather(s32[1,1,32]{2,1,0:T(1,128)S(1)} %bitcast.212), channel_id=1, replica_groups=mesh['parts'=2,'seq'=16] {'seq'}, dimensions={0}, use_global_device_ids=true | all-gather | bytes 2176 | tf_op jit(solution)/shard_map/all_gather | solution.py:60
  49.8 1.6 %reduce.8 = bf16[16,8192]{1,0:T(8,128)(2,1)S(1)} reduce(bf16[16,1,8192]{2,1,0:T(2,128)(2,1)S(1)} %all-gather.1, bf16[]{:T(256)} %constant.83), dimensions={1}, to_apply=%all-gather.1.reduce_sub_computation | reduce | bytes 524290 | tf_op jit(solution)/shard_map/all_gather | solution.py:59
  52.8 1.1 copy-done.2
  54.7 1.9 %copy.116 = bf16[8,8,128,128]{3,2,1,0:T(8,128)(2,1)} copy(bf16[8,8,128,128]{3,0,2,1:T(8,128)(2,1)S(1)} %bitcast_bitcast_fusion.2) | data formatting | bytes 4194304
  56.6 20.4 %while.15 = (s32[]{:T(128)}, f32[8,16,8]{1,2,0:T(8,128)S(1)}, f32[8,16,8]{1,2,0:T(8,128)S(1)}, f32[8,16,8,128]{3,2,0,1:T(8,128)S(1)}, bf16[8,16,8,128]{3,2,0,1:T...) while((s32[]{:T(128)}, f32[8,16,8]{1,2,0:T(8,128)S(1)}, ...), condition=%wide.region_7.8_spmd.clone, body=%wide.region_1.7_spmd.clone.sunk | while | flops 68535040 | bytes 2387621 | solution.py:77
  57.7 1.3 %fusion.67 = f32[16,8,128]{2,0,1:T(8,128)S(1)} fusion(bf16[16,8,8,128]{3,1,2,0:T(8,128)(2,1)S(1)} %get-tuple-element.219, bf16[8,8,128,128]{3,2,1,0:T(8,128)(2,1)} %get-tuple-element.245, s32[]{:T(128)} %get-tuple-element.230, f32[16,8,8]{0,1,2:T(8,128)S(1)} %copy.220), kind=kOutput, calls=%fused_computation.4.clone.1 | convolution fusion | flops 33800192 | bytes 594432 | tf_op jit(solution)/shard_map/while/body/eval_jaxpr/tgbj,bjd->tgbd/dot_general | solution.py:29
  60.2 1.3 %fusion.67 = f32[16,8,128]{2,0,1:T(8,128)S(1)} fusion(bf16[16,8,8,128]{3,1,2,0:T(8,128)(2,1)S(1)} %get-tuple-element.219, bf16[8,8,128,128]{3,2,1,0:T(8,128)(2,1)} %get-tuple-element.245, s32[]{:T(128)} %get-tuple-element.230, f32[16,8,8]{0,1,2:T(8,128)S(1)} %copy.220), kind=kOutput, calls=%fused_computation.4.clone.1 | convolution fusion | flops 33800192 | bytes 594432 | tf_op jit(solution)/shard_map/while/body/eval_jaxpr/tgbj,bjd->tgbd/dot_general | solution.py:29
  62.8 1.3 %fusion.67 = f32[16,8,128]{2,0,1:T(8,128)S(1)} fusion(bf16[16,8,8,128]{3,1,2,0:T(8,128)(2,1)S(1)} %get-tuple-element.219, bf16[8,8,128,128]{3,2,1,0:T(8,128)(2,1)} %get-tuple-element.245, s32[]{:T(128)} %get-tuple-element.230, f32[16,8,8]{0,1,2:T(8,128)S(1)} %copy.220), kind=kOutput, calls=%fused_computation.4.clone.1 | convolution fusion | flops 33800192 | bytes 594432 | tf_op jit(solution)/shard_map/while/body/eval_jaxpr/tgbj,bjd->tgbd/dot_general | solution.py:29
  65.3 1.3 %fusion.67 = f32[16,8,128]{2,0,1:T(8,128)S(1)} fusion(bf16[16,8,8,128]{3,1,2,0:T(8,128)(2,1)S(1)} %get-tuple-element.219, bf16[8,8,128,128]{3,2,1,0:T(8,128)(2,1)} %get-tuple-element.245, s32[]{:T(128)} %get-tuple-element.230, f32[16,8,8]{0,1,2:T(8,128)S(1)} %copy.220), kind=kOutput, calls=%fused_computation.4.clone.1 | convolution fusion | flops 33800192 | bytes 594432 | tf_op jit(solution)/shard_map/while/body/eval_jaxpr/tgbj,bjd->tgbd/dot_general | solution.py:29
  67.8 1.3 %fusion.67 = f32[16,8,128]{2,0,1:T(8,128)S(1)} fusion(bf16[16,8,8,128]{3,1,2,0:T(8,128)(2,1)S(1)} %get-tuple-element.219, bf16[8,8,128,128]{3,2,1,0:T(8,128)(2,1)} %get-tuple-element.245, s32[]{:T(128)} %get-tuple-element.230, f32[16,8,8]{0,1,2:T(8,128)S(1)} %copy.220), kind=kOutput, calls=%fused_computation.4.clone.1 | convolution fusion | flops 33800192 | bytes 594432 | tf_op jit(solution)/shard_map/while/body/eval_jaxpr/tgbj,bjd->tgbd/dot_general | solution.py:29
  70.4 1.3 %fusion.67 = f32[16,8,128]{2,0,1:T(8,128)S(1)} fusion(bf16[16,8,8,128]{3,1,2,0:T(8,128)(2,1)S(1)} %get-tuple-element.219, bf16[8,8,128,128]{3,2,1,0:T(8,128)(2,1)} %get-tuple-element.245, s32[]{:T(128)} %get-tuple-element.230, f32[16,8,8]{0,1,2:T(8,128)S(1)} %copy.220), kind=kOutput, calls=%fused_computation.4.clone.1 | convolution fusion | flops 33800192 | bytes 594432 | tf_op jit(solution)/shard_map/while/body/eval_jaxpr/tgbj,bjd->tgbd/dot_general | solution.py:29
  72.9 1.3 %fusion.67 = f32[16,8,128]{2,0,1:T(8,128)S(1)} fusion(bf16[16,8,8,128]{3,1,2,0:T(8,128)(2,1)S(1)} %get-tuple-element.219, bf16[8,8,128,128]{3,2,1,0:T(8,128)(2,1)} %get-tuple-element.245, s32[]{:T(128)} %get-tuple-element.230, f32[16,8,8]{0,1,2:T(8,128)S(1)} %copy.220), kind=kOutput, calls=%fused_computation.4.clone.1 | convolution fusion | flops 33800192 | bytes 594432 | tf_op jit(solution)/shard_map/while/body/eval_jaxpr/tgbj,bjd->tgbd/dot_general | solution.py:29
  75.5 1.3 %fusion.67 = f32[16,8,128]{2,0,1:T(8,128)S(1)} fusion(bf16[16,8,8,128]{3,1,2,0:T(8,128)(2,1)S(1)} %get-tuple-element.219, bf16[8,8,128,128]{3,2,1,0:T(8,128)(2,1)} %get-tuple-element.245, s32[]{:T(128)} %get-tuple-element.230, f32[16,8,8]{0,1,2:T(8,128)S(1)} %copy.220), kind=kOutput, calls=%fused_computation.4.clone.1 | convolution fusion | flops 33800192 | bytes 594432 | tf_op jit(solution)/shard_map/while/body/eval_jaxpr/tgbj,bjd->tgbd/dot_general | solution.py:29
  77.6 0.7 copy.121
  78.2 3.4 %all-to-all-start = ((f32[16,1,64]{2,1,0:T(1,128)}), f32[16,1,64]{2,1,0:T(1,128)S(1)}, u32[]{:S(2)}, u32[]{:S(2)}) async-start(f32[16,1,64]{2,1,0:T(1,128)} %copy.121), calls=%async_computation | async-start | bytes 16384 | tf_op jit(solution)/shard_map/all_to_all | solution.py:135
  81.7 2.2 %copy.161 = bf16[128,8,8,128]{3,2,1,0:T(8,128)(2,1)S(1)} copy(bf16[128,8,8,128]{3,1,2,0:T(8,128)(2,1)} %bitcast.194) | data formatting | bytes 4194304
  85.7 0.7 copy.125
  86.6 1.4 %all-to-all-done = f32[16,1,64]{2,1,0:T(1,128)S(1)} async-done(((f32[16,1,64]{2,1,0:T(1,128)}), f32[16,1,64]{2,1,0:T(1,128)S(1)}, u32[]{:S(2)}, u32[]{:S(2)}) %all-to-all-start) | async-done | bytes 4128 | tf_op jit(solution)/shard_map/all_to_all | solution.py:135
  88.0 4.6 %all-to-all-start.1 = ((f32[16,1,64]{2,1,0:T(1,128)}), f32[16,1,64]{2,1,0:T(1,128)S(1)}, u32[]{:S(2)}, u32[]{:S(2)}) async-start(f32[16,1,64]{2,1,0:T(1,128)} %copy.125), calls=%async_computation.1 | async-start | bytes 16384 | tf_op jit(solution)/shard_map/all_to_all | solution.py:136
  93.8 2.3 %reduce.15 = bf16[16,8192]{1,0:T(8,128)(2,1)S(1)} reduce(bf16[16,1,8192]{2,1,0:T(2,128)(2,1)S(1)} %reshape.281, bf16[]{:T(256)} %broadcast.113), dimensions={1}, to_apply=%reshape.281.reduce_sub_computation | reduce | bytes 524290 | tf_op jit(solution)/shard_map/reshape | solution.py:139
  96.1 0.9 reshape.294
  97.0 2.0 %all-to-all-done.1 = f32[16,1,64]{2,1,0:T(1,128)S(1)} async-done(((f32[16,1,64]{2,1,0:T(1,128)}), f32[16,1,64]{2,1,0:T(1,128)S(1)}, u32[]{:S(2)}, u32[]{:S(2)}) %all-to-all-start.1) | async-done | bytes 4128 | tf_op jit(solution)/shard_map/all_to_all | solution.py:136
  99.0 4.1 %all-to-all-start.2 = ((bf16[16,2,4096]{2,1,0:T(2,128)(2,1)}), bf16[16,2,4096]{2,1,0:T(2,128)(2,1)S(1)}, u32[]{:S(2)}, u32[]{:S(2)}) async-start(bf16[16,2,4096]{2,1,0:T(2,128)(2,1)} %reshape.294), calls=%async_computation.2 | async-start | bytes 524288 | tf_op jit(solution)/shard_map/all_to_all | solution.py:138
  103.1 9.9 %all-to-all-done.2 = bf16[16,2,4096]{2,1,0:T(2,128)(2,1)S(1)} async-done(((bf16[16,2,4096]{2,1,0:T(2,128)(2,1)}), bf16[16,2,4096]{2,1,0:T(2,128)(2,1)S(1)}, u32[]{:S(2)}, u32[]{:S(2)}) %all-to-all-start.2) | async-done | bytes 262176 | tf_op jit(solution)/shard_map/all_to_all | solution.py:138
  113.5 0.8 multiply_reduce_fusion.1
  114.4 0.7 divide_convert_fusion
  (149 shorter events, 18.6 us)
Async XLA Ops:
  0.0 29.1 %copy-start = (bf16[1,1024]{1,0:T(2,128)(2,1)S(1)}, bf16[1,1024]{1,0:T(2,128)(2,1)}, u32[]{:S(2)}) copy-start(bf16[1,1024]{1,0:T(2,128)(2,1)} %param.12) | copy-start | bytes 6148
  24.8 6.3 %copy-start.8 = (pred[2]{0:T(512)(128)(4,1)}, pred[2]{0:T(512)(128)(4,1)S(1)}, u32[]{:S(2)}) copy-start(pred[2]{0:T(512)(128)(4,1)S(1)} %get-tuple-element.152) | copy-start | bytes 10
  27.1 0.7 copy-start.11
  29.3 2.7 %copy-start.10 = (s32[1,32]{1,0:T(1,128)S(1)}, s32[1,32]{1,0:T(1,128)}, u32[]{:S(2)}) copy-start(s32[1,32]{1,0:T(1,128)} %param.18) | copy-start | bytes 388
  30.1 21.4 %copy-start.1 = (bf16[1024,1024]{1,0:T(8,128)(2,1)S(1)}, bf16[1024,1024]{1,0:T(8,128)(2,1)}, u32[]{:S(2)}) copy-start(bf16[1024,1024]{1,0:T(8,128)(2,1)} %param.14) | copy-start | bytes 6291460
  52.3 1.6 %copy-start.2 = (bf16[1024,1024]{1,0:T(8,128)(2,1)S(1)}, bf16[1024,1024]{1,0:T(8,128)(2,1)}, u32[]{:S(2)}) copy-start(bf16[1024,1024]{1,0:T(8,128)(2,1)} %param.15) | copy-start | bytes 6291460
  54.6 1.9 %copy-start.4 = (f32[8,16,8]{1,2,0:T(8,128)S(1)}, f32[8,16,8]{1,2,0:T(8,128)}, u32[]{:S(2)}) copy-start(f32[8,16,8]{1,2,0:T(8,128)} %custom-call) | copy-start | bytes 12292
  54.7 1.9 %copy-start.5 = (f32[8,16,8]{1,2,0:T(8,128)S(1)}, f32[8,16,8]{1,2,0:T(8,128)}, u32[]{:S(2)}) copy-start(f32[8,16,8]{1,2,0:T(8,128)} %custom-call.1) | copy-start | bytes 12292
  78.2 9.8 %all-to-all-start = ((f32[16,1,64]{2,1,0:T(1,128)}), f32[16,1,64]{2,1,0:T(1,128)S(1)}, u32[]{:S(2)}, u32[]{:S(2)}) async-start(f32[16,1,64]{2,1,0:T(1,128)} %copy.121), calls=%async_computation | async-start | bytes 16384 | tf_op jit(solution)/shard_map/all_to_all | solution.py:135
  83.9 0.7 copy-start.6
  83.9 0.9 copy-start.7
  83.9 1.0 copy-start.3
  84.9 0.7 copy-start.9
  88.0 10.9 %all-to-all-start.1 = ((f32[16,1,64]{2,1,0:T(1,128)}), f32[16,1,64]{2,1,0:T(1,128)S(1)}, u32[]{:S(2)}, u32[]{:S(2)}) async-start(f32[16,1,64]{2,1,0:T(1,128)} %copy.125), calls=%async_computation.1 | async-start | bytes 16384 | tf_op jit(solution)/shard_map/all_to_all | solution.py:136
  99.0 14.1 %all-to-all-start.2 = ((bf16[16,2,4096]{2,1,0:T(2,128)(2,1)}), bf16[16,2,4096]{2,1,0:T(2,128)(2,1)S(1)}, u32[]{:S(2)}, u32[]{:S(2)}) async-start(bf16[16,2,4096]{2,1,0:T(2,128)(2,1)} %reshape.294), calls=%async_computation.2 | async-start | bytes 524288 | tf_op jit(solution)/shard_map/all_to_all | solution.py:138
where the time goes:
time: 116 us; the launch traced here: 115 us
  blocking collectives  42.3 us (36%)
  local copies, waits for them, and re-layouts  18.6 us (16%)
  matrix products  15 us (13%)
  waiting for transfers between devices  13.3 us (11%)
  other arithmetic  13.2 us (11%)
  starting transfers between devices  12 us (10%)
    all_gather x1, blocking collectives, per_device(): gathered = lax.all_gather(queries, 'seq', axis=0, tiled=True)  24.8 us
    all_gather x1, blocking collectives, per_device(): every_list = lax.all_gather(keep_lists, 'seq', axis=0, tiled=True)  17.4 us
    unnamed x33, local copies, waits for them, and re-layouts  11.3 us
    dot_general x9, matrix products, block_terms(): jnp.einsum(form, weights.astype(jnp.bfloat16), value_rows, preferred_elem...  10.7 us
    all_to_all x1, waiting for transfers between devices, per_device(): lax.all_to_all(units.reshape(devices, 1, HEADS * HD), 'seq', split_axis=0...  9.94 us
    reduce_sum x9, other arithmetic, block_terms(): block_sum = jnp.sum(weights, axis=-1)  5.2 us
    all_to_all x1, starting transfers between devices, per_device(): lax.all_to_all(span_sum[:, None, :], 'seq', split_axis=0, concat_axis=1,...  4.56 us
    all_to_all x1, starting transfers between devices, per_device(): lax.all_to_all(units.reshape(devices, 1, HEADS * HD), 'seq', split_axis=0...  4.05 us
  transfers between devices with their start and end apart: 3, of which 3 were waited for; matrix products, arithmetic and copies ran while one was open for 8% of the time, Pallas kernels for 0%

commit v1 on v0

--- a/solution.py
+++ b/solution.py
@@ -57,7 +57,12 @@
     parity = my_index % 2
     blocks_here = doc_keys.shape[0] // BLOCK
     gathered = lax.all_gather(queries, "seq", axis=0, tiled=True)
-    every_list = lax.all_gather(keep_lists, "seq", axis=0, tiled=True)
+    ring = [keep_lists]
+    for hop in range(15):
+        ring.append(lax.ppermute(ring[-1], "seq", [(dev, (dev + 1) % 16) for dev in range(16)]))
+    every_list = jnp.roll(
+        jnp.concatenate(ring[::-1], axis=0), (lax.axis_index("seq") + 1) * ring[0].shape[0], axis=0
+    )
     local_ids = every_list.reshape(devices // 2, -1) - my_index * blocks_here
     block_range = jnp.arange(blocks_here, dtype=jnp.int32)
     row_hits = jnp.any(local_ids[:, :, None] == block_range[None, None, :], axis=1)

time: 116 us -> 180 us (1.55)
  waiting for transfers between devices: 13.3 us -> 91.7 us
  blocking collectives: 42.3 us -> 24.4 us
  local copies, waits for them, and re-layouts: 18.6 us -> 23 us
    ppermute x0 -> x15, waiting for transfers between devices: none -> 74.5 us  [per_device(): lax.ppermute(ring[-1], 'seq', [(dev, (dev + 1) % 16) for dev in range(16)])]
    all_gather x1 -> x0, blocking collectives: 17.4 us -> none  [per_device(): every_list = lax.all_gather(keep_lists, 'seq', axis=0, tiled=True)]
    dot_general x9, matrix products: 10.7 us -> 3.02 us  [block_terms(): jnp.einsum(form, weights.astype(jnp.bfloat16), value_rows, preferred_elem...]
    dot_general x8, matrix products: 3.23 us -> 10.8 us  [doc_head(): jnp.einsum('tgd,bjd->tgbj', q_part, key_part, preferred_element_type=jnp....]
    all_to_all x1, waiting for transfers between devices: 1.45 us -> 5.37 us  [per_device(): lax.all_to_all(span_max[:, None, :], 'seq', split_axis=0, concat_axis=1,...]
    concatenate x0 -> x1, local copies, waits for them, and re-layouts: none -> 2.63 us  [per_device(): jnp.roll(jnp.concatenate(ring[::-1], axis=0), (lax.axis_index('seq') + 1)...]
    unnamed x33 -> x57, local copies, waits for them, and re-layouts: 11.3 us -> 10.7 us
  transfers between devices with their start and end apart: 3 -> 18, of which waited for: 3 -> 17; matrix products, arithmetic and copies ran while one was open for 8% -> 12% of each run, Pallas kernels for 0% -> 0%
where the time goes in v1:
time: 180 us; the launch traced here: 179 us
  waiting for transfers between devices  91.7 us (51%)
  blocking collectives  24.4 us (14%)
  local copies, waits for them, and re-layouts  23 us (13%)
  matrix products  14.9 us (8%)
  other arithmetic  12.6 us (7%)
  starting transfers between devices  11.8 us (7%)
    ppermute x15, waiting for transfers between devices, per_device(): lax.ppermute(ring[-1], 'seq', [(dev, (dev + 1) % 16) for dev in range(16)])  74.5 us
    all_gather x1, blocking collectives, per_device(): gathered = lax.all_gather(queries, 'seq', axis=0, tiled=True)  24.4 us
    dot_general x8, matrix products, doc_head(): jnp.einsum('tgd,bjd->tgbj', q_part, key_part, preferred_element_type=jnp....  10.8 us
    unnamed x57, local copies, waits for them, and re-layouts  10.7 us
    all_to_all x1, waiting for transfers between devices, per_device(): lax.all_to_all(units.reshape(devices, 1, HEADS * HD), 'seq', split_axis=0...  9.94 us
    all_to_all x1, waiting for transfers between devices, per_device(): lax.all_to_all(span_max[:, None, :], 'seq', split_axis=0, concat_axis=1,...  5.37 us
    reduce_sum x9, other arithmetic, block_terms(): block_sum = jnp.sum(weights, axis=-1)  4.68 us
    all_to_all x1, starting transfers between devices, per_device(): lax.all_to_all(units.reshape(devices, 1, HEADS * HD), 'seq', split_axis=0...  3.84 us
  transfers between devices with their start and end apart: 18, of which 17 were waited for; matrix products, arithmetic and copies ran while one was open for 12% of the time, Pallas kernels for 0%

profile of v1, /device:TPU:0, one launch (start us, length us, event | category | flops | bytes accessed | tf_op | source)
XLA Modules:
  0.0 179.2 jit_solution(14356368474589211742)
XLA Ops:
  0.5 24.4 %all-gather = bf16[16,1,8192]{2,1,0:T(2,128)(2,1)S(1)} all-gather(bf16[1,1,8192]{2,1,0:T(2,128)(2,1)} %bitcast.209), channel_id=1, replica_groups=mesh['parts'=2,'seq'=16] {'seq'}, dimensions={0}, use_global_device_ids=true | all-gather | bytes 278528 | tf_op jit(solution)/shard_map/all_gather | solution.py:59
  24.9 2.2 %copy.157 = bf16[128,8,8,128]{3,2,1,0:T(8,128)(2,1)S(1)} copy(bf16[128,8,8,128]{3,1,2,0:T(8,128)(2,1)} %bitcast.190) | data formatting | bytes 4194304
  27.2 1.5 bitcast_bitcast_fusion.3
  30.1 1.4 bitcast_bitcast_fusion.2
  39.9 5.3 %collective-permute-done.1 = s32[1,32]{1,0:T(1,128)S(1)} collective-permute-done((s32[1,32]{1,0:T(1,128)S(1)}, s32[1,32]{1,0:T(1,128)S(1)}, u32[]{:S(2)}, u32[]{:S(2)}) %collective-permute-start.1) | collective-permute-done | bytes 160 | tf_op jit(solution)/shard_map/ppermute | solution.py:62
  45.3 5.7 %collective-permute-done.2 = s32[1,32]{1,0:T(1,128)S(1)} collective-permute-done((s32[1,32]{1,0:T(1,128)S(1)}, s32[1,32]{1,0:T(1,128)S(1)}, u32[]{:S(2)}, u32[]{:S(2)}) %collective-permute-start.2) | collective-permute-done | bytes 160 | tf_op jit(solution)/shard_map/ppermute | solution.py:62
  51.0 5.7 %collective-permute-done.3 = s32[1,32]{1,0:T(1,128)S(1)} collective-permute-done((s32[1,32]{1,0:T(1,128)S(1)}, s32[1,32]{1,0:T(1,128)S(1)}, u32[]{:S(2)}, u32[]{:S(2)}) %collective-permute-start.3) | collective-permute-done | bytes 160 | tf_op jit(solution)/shard_map/ppermute | solution.py:62
  56.7 5.7 %collective-permute-done.4 = s32[1,32]{1,0:T(1,128)S(1)} collective-permute-done((s32[1,32]{1,0:T(1,128)S(1)}, s32[1,32]{1,0:T(1,128)S(1)}, u32[]{:S(2)}, u32[]{:S(2)}) %collective-permute-start.4) | collective-permute-done | bytes 160 | tf_op jit(solution)/shard_map/ppermute | solution.py:62
  62.4 5.8 %collective-permute-done.5 = s32[1,32]{1,0:T(1,128)} collective-permute-done((s32[1,32]{1,0:T(1,128)S(1)}, s32[1,32]{1,0:T(1,128)}, u32[]{:S(2)}, u32[]{:S(2)}) %collective-permute-start.5) | collective-permute-done | bytes 160 | tf_op jit(solution)/shard_map/ppermute | solution.py:62
  68.3 1.6 reduce.8
  69.9 4.1 %collective-permute-done.6 = s32[1,32]{1,0:T(1,128)} collective-permute-done((s32[1,32]{1,0:T(1,128)}, s32[1,32]{1,0:T(1,128)}, u32[]{:S(2)}, u32[]{:S(2)}) %collective-permute-start.6) | collective-permute-done | bytes 160 | tf_op jit(solution)/shard_map/ppermute | solution.py:62
  74.0 5.8 %collective-permute-done.7 = s32[1,32]{1,0:T(1,128)S(1)} collective-permute-done((s32[1,32]{1,0:T(1,128)}, s32[1,32]{1,0:T(1,128)S(1)}, u32[]{:S(2)}, u32[]{:S(2)}) %collective-permute-start.7) | collective-permute-done | bytes 160 | tf_op jit(solution)/shard_map/ppermute | solution.py:62
  79.9 1.9 %copy.115 = bf16[8,8,128,128]{3,2,1,0:T(8,128)(2,1)} copy(bf16[8,8,128,128]{3,0,2,1:T(8,128)(2,1)S(1)} %copy-done.1) | data formatting | bytes 4194304
  82.3 3.2 %collective-permute-done.8 = s32[1,32]{1,0:T(1,128)S(1)} collective-permute-done((s32[1,32]{1,0:T(1,128)S(1)}, s32[1,32]{1,0:T(1,128)S(1)}, u32[]{:S(2)}, u32[]{:S(2)}) %collective-permute-start.8) | collective-permute-done | bytes 160 | tf_op jit(solution)/shard_map/ppermute | solution.py:62
  85.7 5.6 %collective-permute-done.9 = s32[1,32]{1,0:T(1,128)S(1)} collective-permute-done((s32[1,32]{1,0:T(1,128)S(1)}, s32[1,32]{1,0:T(1,128)S(1)}, u32[]{:S(2)}, u32[]{:S(2)}) %collective-permute-start.9) | collective-permute-done | bytes 160 | tf_op jit(solution)/shard_map/ppermute | solution.py:62
  91.4 5.6 %collective-permute-done.10 = s32[1,32]{1,0:T(1,128)S(1)} collective-permute-done((s32[1,32]{1,0:T(1,128)S(1)}, s32[1,32]{1,0:T(1,128)S(1)}, u32[]{:S(2)}, u32[]{:S(2)}) %collective-permute-start.10) | collective-permute-done | bytes 160 | tf_op jit(solution)/shard_map/ppermute | solution.py:62
  97.0 5.6 %collective-permute-done.11 = s32[1,32]{1,0:T(1,128)S(1)} collective-permute-done((s32[1,32]{1,0:T(1,128)S(1)}, s32[1,32]{1,0:T(1,128)S(1)}, u32[]{:S(2)}, u32[]{:S(2)}) %collective-permute-start.11) | collective-permute-done | bytes 160 | tf_op jit(solution)/shard_map/ppermute | solution.py:62
  102.7 5.6 %collective-permute-done.12 = s32[1,32]{1,0:T(1,128)S(1)} collective-permute-done((s32[1,32]{1,0:T(1,128)S(1)}, s32[1,32]{1,0:T(1,128)S(1)}, u32[]{:S(2)}, u32[]{:S(2)}) %collective-permute-start.12) | collective-permute-done | bytes 160 | tf_op jit(solution)/shard_map/ppermute | solution.py:62
  108.6 5.4 %collective-permute-done.13 = s32[1,32]{1,0:T(1,128)S(1)} collective-permute-done((s32[1,32]{1,0:T(1,128)S(1)}, s32[1,32]{1,0:T(1,128)S(1)}, u32[]{:S(2)}, u32[]{:S(2)}) %collective-permute-start.13) | collective-permute-done | bytes 160 | tf_op jit(solution)/shard_map/ppermute | solution.py:62
  114.3 5.4 %collective-permute-done.14 = s32[1,32]{1,0:T(1,128)S(1)} collective-permute-done((s32[1,32]{1,0:T(1,128)S(1)}, s32[1,32]{1,0:T(1,128)S(1)}, u32[]{:S(2)}, u32[]{:S(2)}) %collective-permute-start.14) | collective-permute-done | bytes 160 | tf_op jit(solution)/shard_map/ppermute | solution.py:62
  119.7 2.6 %concatenate.6 = s32[32,32]{1,0:T(8,128)S(1)} concatenate(s32[1,32]{1,0:T(1,128)S(1)} %collective-permute-done.14, s32[1,32]{1,0:T(1,128)S(1)} %collective-permute-done.13, s32[1,32]{1,0:T(1,128)S(1)} %collective-permute-done.12, s32[1,32]{1,0:T(1,128)S(1)} %collective-permute-done.11, s32[1,32]{1,0:T(1,128)S(1)} %collective-permute-done.10, s32[1,32]{1,0:T(1,128)S(1)} %collective-permute-done.9, ...), dimensions={0} | concatenate | bytes 8192 | tf_op jit(solution)/shard_map/jit(_roll_dynamic)/concatenate | solution.py:63
  122.7 20.3 %while.15 = (s32[]{:T(128)}, f32[8,16,8]{1,2,0:T(8,128)S(1)}, f32[8,16,8]{1,2,0:T(8,128)S(1)}, f32[8,16,8,128]{3,2,0,1:T(8,128)S(1)}, bf16[8,16,8,128]{3,2,0,1:T...) while((s32[]{:T(128)}, f32[8,16,8]{1,2,0:T(8,128)S(1)}, ...), condition=%wide.region_7.8_spmd.clone, body=%wide.region_1.7_spmd.clone.sunk | while | flops 68535040 | bytes 2415785 | solution.py:82
  127.8 1.4 select_reduce_fusion.5
  132.9 1.4 select_reduce_fusion.5
  135.4 1.4 select_reduce_fusion.5
  143.7 3.4 %all-to-all-start = ((f32[16,1,64]{2,1,0:T(1,128)}), f32[16,1,64]{2,1,0:T(1,128)S(1)}, u32[]{:S(2)}, u32[]{:S(2)}) async-start(f32[16,1,64]{2,1,0:T(1,128)} %copy.121), calls=%async_computation | async-start | bytes 16384 | tf_op jit(solution)/shard_map/all_to_all | solution.py:140
  148.1 5.4 %all-to-all-done = f32[16,1,64]{2,1,0:T(1,128)S(1)} async-done(((f32[16,1,64]{2,1,0:T(1,128)}), f32[16,1,64]{2,1,0:T(1,128)S(1)}, u32[]{:S(2)}, u32[]{:S(2)}) %all-to-all-start) | async-done | bytes 4128 | tf_op jit(solution)/shard_map/all_to_all | solution.py:140
  153.5 3.7 %all-to-all-start.1 = ((f32[16,1,64]{2,1,0:T(1,128)}), f32[16,1,64]{2,1,0:T(1,128)S(1)}, u32[]{:S(2)}, u32[]{:S(2)}) async-start(f32[16,1,64]{2,1,0:T(1,128)} %copy.125), calls=%async_computation.1 | async-start | bytes 16384 | tf_op jit(solution)/shard_map/all_to_all | solution.py:141
  158.3 2.2 %reduce.11 = bf16[16,8192]{1,0:T(8,128)(2,1)S(1)} reduce(bf16[16,1,8192]{2,1,0:T(2,128)(2,1)S(1)} %reshape.276, bf16[]{:T(256)} %broadcast.108), dimensions={1}, to_apply=%reshape.276.reduce_sub_computation | reduce | bytes 524290 | tf_op jit(solution)/shard_map/reshape | solution.py:144
  161.4 2.0 %all-to-all-done.1 = f32[16,1,64]{2,1,0:T(1,128)S(1)} async-done(((f32[16,1,64]{2,1,0:T(1,128)}), f32[16,1,64]{2,1,0:T(1,128)S(1)}, u32[]{:S(2)}, u32[]{:S(2)}) %all-to-all-start.1) | async-done | bytes 4128 | tf_op jit(solution)/shard_map/all_to_all | solution.py:141
  163.3 3.8 %all-to-all-start.2 = ((bf16[16,2,4096]{2,1,0:T(2,128)(2,1)}), bf16[16,2,4096]{2,1,0:T(2,128)(2,1)S(1)}, u32[]{:S(2)}, u32[]{:S(2)}) async-start(bf16[16,2,4096]{2,1,0:T(2,128)(2,1)} %reshape.282), calls=%async_computation.2 | async-start | bytes 524288 | tf_op jit(solution)/shard_map/all_to_all | solution.py:143
  167.2 9.9 %all-to-all-done.2 = bf16[16,2,4096]{2,1,0:T(2,128)(2,1)S(1)} async-done(((bf16[16,2,4096]{2,1,0:T(2,128)(2,1)}), bf16[16,2,4096]{2,1,0:T(2,128)(2,1)S(1)}, u32[]{:S(2)}, u32[]{:S(2)}) %all-to-all-start.2) | async-done | bytes 262176 | tf_op jit(solution)/shard_map/all_to_all | solution.py:143
  (203 shorter events, 33.9 us)
Async XLA Ops:
  0.0 35.0 %copy-start = (bf16[1,1024]{1,0:T(2,128)(2,1)S(1)}, bf16[1,1024]{1,0:T(2,128)(2,1)}, u32[]{:S(2)}) copy-start(bf16[1,1024]{1,0:T(2,128)(2,1)} %param.12) | copy-start | bytes 6148
  0.0 39.6 %collective-permute-start = (s32[1,32]{1,0:T(1,128)}, s32[1,32]{1,0:T(1,128)S(1)}, u32[]{:S(2)}, u32[]{:S(2)}) collective-permute-start(s32[1,32]{1,0:T(1,128)} %param.18), channel_id=1, source_target_pairs={{0,1},{1,2},{2,3},{3,4},{4,5},{5,6},{6,7},{7,8},{8,9},{9,10},{10,1... | collective-permute-start | bytes 392 | tf_op jit(solution)/shard_map/ppermute | solution.py:62
  38.2 41.6 %copy-start.1 = (bf16[8,8,128,128]{3,0,2,1:T(8,128)(2,1)S(1)}, bf16[8,8,128,128]{3,0,2,1:T(8,128)(2,1)}, u32[]{:S(2)}) copy-start(bf16[8,8,128,128]{3,0,2,1:T(8,128)(2,1)} %bitcast_bitcast_fusion.3) | copy-start | bytes 6291460
  39.6 28.6 %copy-start.12 = (s32[1,32]{1,0:T(1,128)}, s32[1,32]{1,0:T(1,128)S(1)}, u32[]{:S(2)}) copy-start(s32[1,32]{1,0:T(1,128)S(1)} %collective-permute-done) | copy-start | bytes 388
  39.6 5.7 %collective-permute-start.1 = (s32[1,32]{1,0:T(1,128)S(1)}, s32[1,32]{1,0:T(1,128)S(1)}, u32[]{:S(2)}, u32[]{:S(2)}) collective-permute-start(s32[1,32]{1,0:T(1,128)S(1)} %collective-permute-done), channel_id=1, source_target_pairs={{0,1},{1,2},{2,3},{3,4},{4,5},{5,6},{6,7},{7,8},{8,9},{9,10},{10,1... | collective-permute-start | bytes 392 | tf_op jit(solution)/shard_map/ppermute | solution.py:62
  45.3 22.9 %copy-start.14 = (s32[1,32]{1,0:T(1,128)}, s32[1,32]{1,0:T(1,128)S(1)}, u32[]{:S(2)}) copy-start(s32[1,32]{1,0:T(1,128)S(1)} %collective-permute-done.1) | copy-start | bytes 388
  45.3 5.7 %collective-permute-start.2 = (s32[1,32]{1,0:T(1,128)S(1)}, s32[1,32]{1,0:T(1,128)S(1)}, u32[]{:S(2)}, u32[]{:S(2)}) collective-permute-start(s32[1,32]{1,0:T(1,128)S(1)} %collective-permute-done.1), channel_id=1, source_target_pairs={{0,1},{1,2},{2,3},{3,4},{4,5},{5,6},{6,7},{7,8},{8,9},{9,10},{10,1... | collective-permute-start | bytes 392 | tf_op jit(solution)/shard_map/ppermute | solution.py:62
  51.0 17.2 %copy-start.16 = (s32[1,32]{1,0:T(1,128)}, s32[1,32]{1,0:T(1,128)S(1)}, u32[]{:S(2)}) copy-start(s32[1,32]{1,0:T(1,128)S(1)} %collective-permute-done.2) | copy-start | bytes 388
  51.0 5.7 %collective-permute-start.3 = (s32[1,32]{1,0:T(1,128)S(1)}, s32[1,32]{1,0:T(1,128)S(1)}, u32[]{:S(2)}, u32[]{:S(2)}) collective-permute-start(s32[1,32]{1,0:T(1,128)S(1)} %collective-permute-done.2), channel_id=1, source_target_pairs={{0,1},{1,2},{2,3},{3,4},{4,5},{5,6},{6,7},{7,8},{8,9},{9,10},{10,1... | collective-permute-start | bytes 392 | tf_op jit(solution)/shard_map/ppermute | solution.py:62
  56.7 5.7 %collective-permute-start.4 = (s32[1,32]{1,0:T(1,128)S(1)}, s32[1,32]{1,0:T(1,128)S(1)}, u32[]{:S(2)}, u32[]{:S(2)}) collective-permute-start(s32[1,32]{1,0:T(1,128)S(1)} %collective-permute-done.3), channel_id=1, source_target_pairs={{0,1},{1,2},{2,3},{3,4},{4,5},{5,6},{6,7},{7,8},{8,9},{9,10},{10,1... | collective-permute-start | bytes 392 | tf_op jit(solution)/shard_map/ppermute | solution.py:62
  62.4 5.8 %collective-permute-start.5 = (s32[1,32]{1,0:T(1,128)S(1)}, s32[1,32]{1,0:T(1,128)}, u32[]{:S(2)}, u32[]{:S(2)}) collective-permute-start(s32[1,32]{1,0:T(1,128)S(1)} %collective-permute-done.4), channel_id=1, source_target_pairs={{0,1},{1,2},{2,3},{3,4},{4,5},{5,6},{6,7},{7,8},{8,9},{9,10},{10,1... | collective-permute-start | bytes 392 | tf_op jit(solution)/shard_map/ppermute | solution.py:62
  68.2 5.8 %collective-permute-start.6 = (s32[1,32]{1,0:T(1,128)}, s32[1,32]{1,0:T(1,128)}, u32[]{:S(2)}, u32[]{:S(2)}) collective-permute-start(s32[1,32]{1,0:T(1,128)} %collective-permute-done.5), channel_id=1, source_target_pairs={{0,1},{1,2},{2,3},{3,4},{4,5},{5,6},{6,7},{7,8},{8,9},{9,10},{10,1... | collective-permute-start | bytes 392 | tf_op jit(solution)/shard_map/ppermute | solution.py:62
  73.9 5.9 %collective-permute-start.7 = (s32[1,32]{1,0:T(1,128)}, s32[1,32]{1,0:T(1,128)S(1)}, u32[]{:S(2)}, u32[]{:S(2)}) collective-permute-start(s32[1,32]{1,0:T(1,128)} %collective-permute-done.6), channel_id=1, source_target_pairs={{0,1},{1,2},{2,3},{3,4},{4,5},{5,6},{6,7},{7,8},{8,9},{9,10},{10,1... | collective-permute-start | bytes 392 | tf_op jit(solution)/shard_map/ppermute | solution.py:62
  79.8 5.7 %collective-permute-start.8 = (s32[1,32]{1,0:T(1,128)S(1)}, s32[1,32]{1,0:T(1,128)S(1)}, u32[]{:S(2)}, u32[]{:S(2)}) collective-permute-start(s32[1,32]{1,0:T(1,128)S(1)} %collective-permute-done.7), channel_id=1, source_target_pairs={{0,1},{1,2},{2,3},{3,4},{4,5},{5,6},{6,7},{7,8},{8,9},{9,10},{10,1... | collective-permute-start | bytes 392 | tf_op jit(solution)/shard_map/ppermute | solution.py:62
  81.7 15.2 %copy-start.9 = (f32[2,8,8]{2,1,0:T(8,128)S(1)}, f32[2,8,8]{2,1,0:T(8,128)}, u32[]{:S(2)}) copy-start(f32[2,8,8]{2,1,0:T(8,128)} %get-tuple-element.139) | copy-start | bytes 1540
  81.7 20.9 %copy-start.8 = (f32[2,8,8]{2,1,0:T(8,128)S(1)}, f32[2,8,8]{2,1,0:T(8,128)}, u32[]{:S(2)}) copy-start(f32[2,8,8]{2,1,0:T(8,128)} %get-tuple-element.138) | copy-start | bytes 1540
  81.7 37.9 %copy-start.11 = (s32[1,32]{1,0:T(1,128)S(1)}, s32[1,32]{1,0:T(1,128)}, u32[]{:S(2)}) copy-start(s32[1,32]{1,0:T(1,128)} %param.18) | copy-start | bytes 388
  81.8 37.9 %copy-start.13 = (s32[1,32]{1,0:T(1,128)S(1)}, s32[1,32]{1,0:T(1,128)}, u32[]{:S(2)}) copy-start(s32[1,32]{1,0:T(1,128)} %copy-done.12) | copy-start | bytes 388
  81.8 37.9 %copy-start.15 = (s32[1,32]{1,0:T(1,128)S(1)}, s32[1,32]{1,0:T(1,128)}, u32[]{:S(2)}) copy-start(s32[1,32]{1,0:T(1,128)} %copy-done.14) | copy-start | bytes 388
  81.8 37.9 %copy-start.17 = (s32[1,32]{1,0:T(1,128)S(1)}, s32[1,32]{1,0:T(1,128)}, u32[]{:S(2)}) copy-start(s32[1,32]{1,0:T(1,128)} %copy-done.16) | copy-start | bytes 388
  81.8 37.9 %copy-start.19 = (s32[1,32]{1,0:T(1,128)S(1)}, s32[1,32]{1,0:T(1,128)}, u32[]{:S(2)}) copy-start(s32[1,32]{1,0:T(1,128)} %copy-done.18) | copy-start | bytes 388
  81.8 37.9 %copy-start.21 = (s32[1,32]{1,0:T(1,128)S(1)}, s32[1,32]{1,0:T(1,128)}, u32[]{:S(2)}) copy-start(s32[1,32]{1,0:T(1,128)} %copy-done.20) | copy-start | bytes 388
  81.8 40.9 %copy-start.6 = (f32[8,16,8]{1,2,0:T(8,128)S(1)}, f32[8,16,8]{1,2,0:T(8,128)}, u32[]{:S(2)}) copy-start(f32[8,16,8]{1,2,0:T(8,128)} %custom-call.1) | copy-start | bytes 12292
  85.5 5.7 %collective-permute-start.9 = (s32[1,32]{1,0:T(1,128)S(1)}, s32[1,32]{1,0:T(1,128)S(1)}, u32[]{:S(2)}, u32[]{:S(2)}) collective-permute-start(s32[1,32]{1,0:T(1,128)S(1)} %collective-permute-done.8), channel_id=1, source_target_pairs={{0,1},{1,2},{2,3},{3,4},{4,5},{5,6},{6,7},{7,8},{8,9},{9,10},{10,1... | collective-permute-start | bytes 392 | tf_op jit(solution)/shard_map/ppermute | solution.py:62
  91.2 5.7 %collective-permute-start.10 = (s32[1,32]{1,0:T(1,128)S(1)}, s32[1,32]{1,0:T(1,128)S(1)}, u32[]{:S(2)}, u32[]{:S(2)}) collective-permute-start(s32[1,32]{1,0:T(1,128)S(1)} %collective-permute-done.9), channel_id=1, source_target_pairs={{0,1},{1,2},{2,3},{3,4},{4,5},{5,6},{6,7},{7,8},{8,9},{9,10},{10,1... | collective-permute-start | bytes 392 | tf_op jit(solution)/shard_map/ppermute | solution.py:62
  96.9 5.7 %collective-permute-start.11 = (s32[1,32]{1,0:T(1,128)S(1)}, s32[1,32]{1,0:T(1,128)S(1)}, u32[]{:S(2)}, u32[]{:S(2)}) collective-permute-start(s32[1,32]{1,0:T(1,128)S(1)} %collective-permute-done.10), channel_id=1, source_target_pairs={{0,1},{1,2},{2,3},{3,4},{4,5},{5,6},{6,7},{7,8},{8,9},{9,10},{10,1... | collective-permute-start | bytes 392 | tf_op jit(solution)/shard_map/ppermute | solution.py:62
  102.6 5.7 %collective-permute-start.12 = (s32[1,32]{1,0:T(1,128)S(1)}, s32[1,32]{1,0:T(1,128)S(1)}, u32[]{:S(2)}, u32[]{:S(2)}) collective-permute-start(s32[1,32]{1,0:T(1,128)S(1)} %collective-permute-done.11), channel_id=1, source_target_pairs={{0,1},{1,2},{2,3},{3,4},{4,5},{5,6},{6,7},{7,8},{8,9},{9,10},{10,1... | collective-permute-start | bytes 392 | tf_op jit(solution)/shard_map/ppermute | solution.py:62
  108.3 5.7 %collective-permute-start.13 = (s32[1,32]{1,0:T(1,128)S(1)}, s32[1,32]{1,0:T(1,128)S(1)}, u32[]{:S(2)}, u32[]{:S(2)}) collective-permute-start(s32[1,32]{1,0:T(1,128)S(1)} %collective-permute-done.12), channel_id=1, source_target_pairs={{0,1},{1,2},{2,3},{3,4},{4,5},{5,6},{6,7},{7,8},{8,9},{9,10},{10,1... | collective-permute-start | bytes 392 | tf_op jit(solution)/shard_map/ppermute | solution.py:62
  114.0 5.7 %collective-permute-start.14 = (s32[1,32]{1,0:T(1,128)S(1)}, s32[1,32]{1,0:T(1,128)S(1)}, u32[]{:S(2)}, u32[]{:S(2)}) collective-permute-start(s32[1,32]{1,0:T(1,128)S(1)} %collective-permute-done.13), channel_id=1, source_target_pairs={{0,1},{1,2},{2,3},{3,4},{4,5},{5,6},{6,7},{7,8},{8,9},{9,10},{10,1... | collective-permute-start | bytes 392 | tf_op jit(solution)/shard_map/ppermute | solution.py:62
  143.7 9.8 %all-to-all-start = ((f32[16,1,64]{2,1,0:T(1,128)}), f32[16,1,64]{2,1,0:T(1,128)S(1)}, u32[]{:S(2)}, u32[]{:S(2)}) async-start(f32[16,1,64]{2,1,0:T(1,128)} %copy.121), calls=%async_computation | async-start | bytes 16384 | tf_op jit(solution)/shard_map/all_to_all | solution.py:140
  153.5 9.8 %all-to-all-start.1 = ((f32[16,1,64]{2,1,0:T(1,128)}), f32[16,1,64]{2,1,0:T(1,128)S(1)}, u32[]{:S(2)}, u32[]{:S(2)}) async-start(f32[16,1,64]{2,1,0:T(1,128)} %copy.125), calls=%async_computation.1 | async-start | bytes 16384 | tf_op jit(solution)/shard_map/all_to_all | solution.py:141
  163.3 13.9 %all-to-all-start.2 = ((bf16[16,2,4096]{2,1,0:T(2,128)(2,1)}), bf16[16,2,4096]{2,1,0:T(2,128)(2,1)S(1)}, u32[]{:S(2)}, u32[]{:S(2)}) async-start(bf16[16,2,4096]{2,1,0:T(2,128)(2,1)} %reshape.282), calls=%async_computation.2 | async-start | bytes 524288 | tf_op jit(solution)/shard_map/all_to_all | solution.py:143
  (10 other events, 42.3 us)
